TPU v7x, 128 devices: a whole 4x4x4 slice. The times are simulated.
128 devices in a mesh: dp: 8 (over y, core), ctx: 16 (over z, x).
Axes of the slice: x: 4, y: 4, z: 4, core: 2. Of those that a mesh axis runs over, the one named last changes fastest.
Arguments:
- queries: bfloat16 [8, 4096, 256], P('dp', 'ctx'), may hold values from -6 to 6
- keys: bfloat16 [8, 4096, 256], P('dp', 'ctx'), may hold values from -6 to 6
- values: bfloat16 [8, 4096, 256], P('dp', 'ctx'), may hold values from -6 to 6
- grad_out: bfloat16 [8, 4096, 256], P('dp', 'ctx'), may hold values from -6 to 6
- log_norm: float32 [8, 2, 4096], P('dp', None, 'ctx'), may hold values from 5 to 7
- offsets: int32 [2, 5], replicated, may hold values from 0 to 15
- q_gain: float32 [256], replicated, may hold values from 0.5 to 2
Outputs:
- grad_queries: bfloat16 [8, 4096, 256], P('dp', 'ctx')
- grad_keys: bfloat16 [8, 4096, 256], P('dp', 'ctx')
- grad_values: bfloat16 [8, 4096, 256], P('dp', 'ctx')
- grad_gain: float32 [256], replicated
All inputs are finite; a program needn't handle non-finite values.
Results may differ from a plain program's by a relative error of at most 0.013.
The roundings to bfloat16 on the way count: a program that leaves them out, or rounds other values in their place, can miss the bound.
Values may be sent and summed in bfloat16 or wider, within the bound.
No kernel may reach another device: no remote copies, remote signals or barrier semaphores. Data moves between devices by JAX's collectives and lax.ppermute only.
A program may use at most 64 MiB of HBM per device.

v0:
```python
import math
import jax
import jax.numpy as jnp
from jax import lax
from jax.sharding import PartitionSpec as P

BLOCK = 128
LEVELS = 5


def swapped(block, axis, stride):
    count = lax.axis_size(axis)
    route = []
    for low in range(count):
        high = low | 1 << stride
        if high != low and high < count:
            route += [(low, high), (high, low)]
    return lax.ppermute(block, axis, route)


def slot_table(device_local, offset_vec, stride, block_count):
    slot_count = (block_count + stride - 1) // stride
    base_block = device_local * block_count + jnp.zeros_like(offset_vec)
    first_step = jnp.maximum((base_block - offset_vec + stride - 1) // stride, 0)
    step_index = first_step[..., None] + jnp.arange(slot_count, dtype=jnp.int32)
    global_block = offset_vec[..., None] + stride * step_index
    local_block = global_block - base_block[..., None]
    usable = (step_index < block_count) & (local_block >= 0) & (local_block < block_count)
    return (jnp.clip(local_block, 0, block_count - 1), usable.astype(jnp.float32))


def segment_slots(shift_vec, span_len, block_count):
    device_col = jnp.arange(span_len, dtype=jnp.int32)[:, None]
    seg_block, seg_usable = slot_table(device_col, shift_vec[None, :], span_len, block_count)
    return (seg_block.transpose(1, 0, 2), seg_usable.transpose(1, 0, 2))


def select_table(local_block, block_count):
    return (local_block[..., None] == jnp.arange(block_count, dtype=jnp.int32)).astype(jnp.float32)


def pick_blocks(data, table):
    head_count, block_count = (data.shape[0], data.shape[1])
    flat = data.reshape(head_count, block_count, -1).astype(jnp.float32)
    chosen = jnp.einsum(
        "hsb,hbx->hsx",
        table,
        flat,
        precision=lax.Precision.HIGHEST,
        preferred_element_type=jnp.float32,
    ).astype(data.dtype)
    return chosen.reshape((head_count, -1) + data.shape[3:])


def place_rows(accum, contrib, table, usable):
    head_count, block_count = (accum.shape[0], accum.shape[1])
    slot_count = table.shape[1]
    weights = table * usable[..., None]
    shaped = contrib.reshape(head_count, slot_count, -1)
    added = jnp.einsum(
        "hsb,hsx->hbx",
        weights,
        shaped,
        precision=lax.Precision.HIGHEST,
        preferred_element_type=jnp.float32,
    )
    return accum + added.reshape(accum.shape)


def attend(
    query_rows,
    dout_rows,
    norm_rows,
    query_mask,
    key_rows,
    value_rows,
    key_mask,
    score_scale,
    row_block,
):
    head_count, query_count, head_dim = query_rows.shape
    steps = query_count // row_block

    def split(array):
        return jnp.moveaxis(array.reshape((head_count, steps, row_block) + array.shape[2:]), 1, 0)

    def step_fn(carry, parts):
        query_blk, dout_blk, norm_blk, mask_blk = parts
        scores = (
            jnp.einsum("hqd,hkd->hqk", query_blk, key_rows, preferred_element_type=jnp.float32)
            * score_scale
        )
        probs = jnp.exp(scores - norm_blk[:, :, None]) * mask_blk[:, :, None] * key_mask[:, None, :]
        probs_low = probs.astype(jnp.bfloat16)
        prob_grad = jnp.einsum(
            "hqd,hkd->hqk", dout_blk, value_rows, preferred_element_type=jnp.float32
        )
        dscore = (probs * prob_grad).astype(jnp.bfloat16)
        query_grad = (
            jnp.einsum("hqk,hkd->hqd", dscore, key_rows, preferred_element_type=jnp.float32)
            * score_scale
        )
        key_part = (
            jnp.einsum("hqk,hqd->hkd", dscore, query_blk, preferred_element_type=jnp.float32)
            * score_scale
        )
        value_part = jnp.einsum(
            "hqk,hqd->hkd", probs_low, dout_blk, preferred_element_type=jnp.float32
        )
        return ((carry[0] + key_part, carry[1] + value_part), query_grad)

    start = jnp.zeros((head_count, key_rows.shape[1], head_dim), jnp.float32)
    totals, query_parts = lax.scan(
        step_fn,
        (start, start),
        (split(query_rows), split(dout_rows), split(norm_rows), split(query_mask)),
    )
    query_grad = jnp.moveaxis(query_parts, 0, 1).reshape(head_count, query_count, head_dim)
    return (query_grad, totals[0], totals[1])


def swap_up(payload, my_index, bit_total):
    for bit_idx in range(bit_total):
        partner = swapped(payload, "ctx", bit_idx)
        lower_half = my_index >> bit_idx & 1 == 0
        payload = jnp.where(
            lower_half,
            jnp.concatenate([payload, partner], axis=1),
            jnp.concatenate([partner, payload], axis=1),
        )
    return payload


def swap_down(sums_kv, my_index, bit_total):
    head_count = sums_kv.shape[0]
    for bit_idx in reversed(range(bit_total)):
        halves = sums_kv.reshape(head_count, 2, -1, sums_kv.shape[-1])
        lower_half = my_index >> bit_idx & 1 == 0
        kept_half = jnp.where(lower_half, halves[:, 0], halves[:, 1])
        sent_half = jnp.where(lower_half, halves[:, 1], halves[:, 0])
        sums_kv = kept_half + swapped(sent_half.astype(jnp.bfloat16), "ctx", bit_idx).astype(
            sent_half.dtype
        )
    return sums_kv


def body(queries, keys, values, grad_out, log_norm, offsets, q_gain):
    query_raw = queries[0]
    token_count, proj_width = query_raw.shape
    head_count = log_norm.shape[1]
    head_dim = proj_width // head_count
    block_count = token_count // BLOCK
    ctx_size = lax.axis_size("ctx")
    score_scale = head_dim ** (-0.5)
    scaled = (query_raw.astype(jnp.float32) * q_gain).astype(jnp.bfloat16)

    def heads(matrix):
        return (
            matrix.reshape(token_count, head_count, head_dim)
            .transpose(1, 0, 2)
            .reshape(head_count, block_count, BLOCK, head_dim)
        )

    query_all = heads(scaled)
    key_all = heads(keys[0])
    value_all = heads(values[0])
    dout_all = heads(grad_out[0])
    norm_all = log_norm[0].reshape(head_count, block_count, BLOCK)
    query_acc = jnp.zeros((head_count, block_count, BLOCK, head_dim), jnp.float32)
    kv_acc = jnp.zeros((head_count, block_count, BLOCK, 2 * head_dim), jnp.float32)
    my_index = lax.axis_index("ctx")
    for level_idx in range(LEVELS):
        span_len = min(2**level_idx, ctx_size)
        shift_vec = offsets[:, level_idx] % span_len
        local_block, usable = slot_table(my_index % span_len, shift_vec, span_len, block_count)
        table = select_table(local_block, block_count)
        slot_count = local_block.shape[1]
        row_block = BLOCK * math.gcd(slot_count, max(1, 512 // BLOCK))
        query_own = pick_blocks(query_all, table)
        dout_own = pick_blocks(dout_all, table)
        norm_own = pick_blocks(norm_all, table)
        mask_own = jnp.repeat(usable, BLOCK, axis=1)
        payload = jnp.concatenate(
            [pick_blocks(key_all, table), pick_blocks(value_all, table)], axis=2
        )
        bit_total = span_len.bit_length() - 1
        payload = swap_up(payload, my_index, bit_total)
        seg_block, seg_usable = segment_slots(shift_vec, span_len, block_count)
        seg_mask = jnp.repeat(seg_usable.reshape(head_count, -1), BLOCK, axis=1)
        level_query, level_key, level_value = attend(
            query_own,
            dout_own,
            norm_own,
            mask_own,
            payload[..., :head_dim],
            payload[..., head_dim:],
            seg_mask,
            score_scale,
            row_block,
        )
        sums_kv = jnp.concatenate([level_key, level_value], axis=2)
        sums_kv = swap_down(sums_kv, my_index, bit_total)
        query_acc = place_rows(query_acc, level_query, table, usable)
        kv_acc = place_rows(kv_acc, sums_kv, table, usable)

    def to_rows(field_acc):
        return (
            field_acc.reshape(head_count, token_count, -1)
            .transpose(1, 0, 2)
            .reshape(token_count, -1)
        )

    dq_rows = to_rows(query_acc)
    grad_queries = (dq_rows * q_gain).astype(jnp.bfloat16)
    grad_keys = to_rows(kv_acc[..., :head_dim]).astype(jnp.bfloat16)
    grad_values = to_rows(kv_acc[..., head_dim:]).astype(jnp.bfloat16)
    gain_total = lax.psum(jnp.sum(query_raw.astype(jnp.float32) * dq_rows, axis=0), ("dp", "ctx"))
    return (grad_queries[None], grad_keys[None], grad_values[None], gain_total)


def solution(mesh):
    in_specs = (
        P("dp", "ctx", None),
        P("dp", "ctx", None),
        P("dp", "ctx", None),
        P("dp", "ctx", None),
        P("dp", None, "ctx"),
        P(),
        P(),
    )
    out_specs = (P("dp", "ctx", None), P("dp", "ctx", None), P("dp", "ctx", None), P())
    return jax.shard_map(body, mesh=mesh, in_specs=in_specs, out_specs=out_specs, check_vma=False)
```

profile of v0, /device:TPU:0, one launch (start us, length us, event | category | flops | bytes accessed | tf_op | source)
XLA Modules:
  0.0 272.5 jit_solution(3529592541120777040)
XLA Ops:
  0.7 0.9 reshape_squeeze.12
  1.7 1.7 clamp_reduce_fusion.3
  3.9 0.9 reshape_squeeze.15
  5.4 1.6 collective-permute-start
  9.4 1.6 collective-permute-start.3
  11.9 1.1 collective-permute-start.6
  19.4 0.9 fusion.193
  20.3 0.9 fusion.203
  26.8 1.0 copy.380
  28.0 0.9 reshape_reshape_transpose.2
  28.9 1.2 reshape.1667
  33.0 0.8 copy-done.5
  34.6 3.2 %collective-permute-start.2 = (bf16[2,256,256]{2,1,0:T(8,128)(2,1)S(1)}, bf16[2,256,256]{2,1,0:T(8,128)(2,1)S(1)}, u32[]{:S(2)}, u32[]{:S(2)}) collective-permute-start(bf16[2,256,256]{2,1,0:T(8,128)(2,1)S(1)} %maximum_select_fusion.7), channel_id=1, source_target_pairs={{0,2},{2,0},{1,3},{3,1},{4,6},{6,4},{5,7},{7,5},{8,10},{10,8},{9,1... | collective-permute-start | bytes 786440 | tf_op jit(solution)/shard_map/ppermute | solution.py:18
  37.9 0.8 copy.373
  39.3 0.8 maximum_select_fusion.9
  40.1 2.0 collective-permute-start.7
  42.1 0.8 maximum_select_fusion.8
  42.9 1.5 collective-permute-start.4
  44.5 1.0 collective-permute-done.2
  47.9 9.2 %collective-permute-done.4 = bf16[2,256,256]{2,1,0:T(8,128)(2,1)} collective-permute-done((bf16[2,256,256]{2,1,0:T(8,128)(2,1)}, bf16[2,256,256]{2,1,0:T(8,128)(2,1)}, u32[]{:S(2)}, u32[]{:S(2)}) %collective-permute-start.4) | collective-permute-done | bytes 262176 | tf_op jit(solution)/shard_map/ppermute | solution.py:18
  57.1 1.3 maximum_select_fusion.4
  58.4 2.4 collective-permute-start.5
  60.8 0.8 fusion.213
  62.4 0.8 fusion.49
  63.1 3.0 %collective-permute-start.11 = (bf16[2,256,256]{2,1,0:T(8,128)(2,1)}, bf16[2,256,256]{2,1,0:T(8,128)(2,1)}, u32[]{:S(2)}, u32[]{:S(2)}) collective-permute-start(bf16[2,256,256]{2,1,0:T(8,128)(2,1)} %fusion.49), channel_id=1, source_target_pairs={{0,2},{2,0},{1,3},{3,1},{4,6},{6,4},{5,7},{7,5},{8,10},{10,8},{9,1... | collective-permute-start | bytes 786440 | tf_op jit(solution)/shard_map/ppermute | solution.py:18
  66.1 2.2 maximum_select_fusion.5
  68.4 4.8 %collective-permute-done.5 = bf16[2,512,256]{2,1,0:T(8,128)(2,1)} collective-permute-done((bf16[2,512,256]{2,1,0:T(8,128)(2,1)S(1)}, bf16[2,512,256]{2,1,0:T(8,128)(2,1)}, u32[]{:S(2)}, u32[]{:S(2)}) %collective-permute-start.5) | collective-permute-done | bytes 524320 | tf_op jit(solution)/shard_map/ppermute | solution.py:18
  73.2 1.4 maximum_select_fusion.1
  77.0 1.5 pad_maximum_fusion.1
  78.5 3.0 %reshape.1673 = f32[2,2,512,256]{2,1,3,0:T(2,128)S(1)} reshape(f32[2,1024,256]{1,2,0:T(8,128)} %pad_maximum_fusion.1) | data formatting | bytes 4194304 | tf_op jit(solution)/shard_map/reshape | solution.py:137
  81.6 2.9 %fusion.212 = (f32[2,1,512,256]{2,1,3,0:T(1,128)}, f32[2,1,512,256]{2,1,3,0:T(1,128)}) fusion(f32[2,2,512,256]{2,1,3,0:T(2,128)S(1)} %reshape.1673), kind=kLoop, calls=%fused_computation.413 | loop fusion | bytes 4194304 | tf_op jit(solution)/shard_map/slice | solution.py:139
  84.5 2.3 copy.151
  86.9 2.4 copy.152
  89.4 2.7 collective-permute-start.13
  92.1 1.8 maximum_select_fusion.2
  93.8 3.7 %collective-permute-start.9 = (bf16[2,1024,256]{2,1,0:T(8,128)(2,1)S(1)}, bf16[2,1024,256]{2,1,0:T(8,128)(2,1)S(1)}, u32[]{:S(2)}, u32[]{:S(2)}) collective-permute-start(bf16[2,1024,256]{2,1,0:T(8,128)(2,1)S(1)} %maximum_select_fusion.2), channel_id=1, source_target_pairs={{0,8},{8,0},{1,9},{9,1},{2,10},{10,2},{3,11},{11,3},{4,12},{12,4},... | collective-permute-start | bytes 3145736 | tf_op jit(solution)/shard_map/ppermute | solution.py:18
  97.5 1.0 fusion.58
  98.5 0.9 copy.191
  99.4 1.0 bitcast_add_fusion.5
  100.4 0.7 fusion.68
  101.1 1.7 collective-permute-start.12
  102.8 2.1 collective-permute-done.13
  105.2 18.4 %collective-permute-done.9 = bf16[2,1024,256]{2,1,0:T(8,128)(2,1)S(1)} collective-permute-done((bf16[2,1024,256]{2,1,0:T(8,128)(2,1)S(1)}, bf16[2,1024,256]{2,1,0:T(8,128)(2,1)S(1)}, u32[]{:S(2)}, u32[]{:S(2)}) %collective-permute-start.9) | collective-permute-done | bytes 1048608 | tf_op jit(solution)/shard_map/ppermute | solution.py:18
  127.4 2.5 pad_maximum_fusion
  129.9 6.6 %reshape.1677 = f32[2,2,1024,256]{2,1,3,0:T(2,128)} reshape(f32[2,2048,256]{1,2,0:T(8,128)} %pad_maximum_fusion) | data formatting | bytes 8388608 | tf_op jit(solution)/shard_map/reshape | solution.py:137
  136.5 9.1 %fusion.211 = (f32[2,1,1024,256]{2,1,3,0:T(1,128)}, f32[2,1,1024,256]{2,1,3,0:T(1,128)}) fusion(f32[2,2,1024,256]{2,1,3,0:T(2,128)} %reshape.1677), kind=kLoop, calls=%fused_computation.412 | loop fusion | bytes 8388608 | tf_op jit(solution)/shard_map/slice | solution.py:139
  145.6 4.6 %copy.157 = f32[2,1,1024,256]{3,2,0,1:T(8,128)S(1)} copy(f32[2,1,1024,256]{2,1,3,0:T(1,128)} %get-tuple-element.141) | data formatting | bytes 4194304
  150.2 6.0 %copy.158 = f32[2,1,1024,256]{3,2,0,1:T(8,128)} copy(f32[2,1,1024,256]{2,1,3,0:T(1,128)} %get-tuple-element.142) | data formatting | bytes 4194304
  156.2 1.9 fusion.36
  158.3 3.1 %collective-permute-start.14 = (bf16[2,256,256]{2,1,0:T(8,128)(2,1)S(1)}, bf16[2,256,256]{2,1,0:T(8,128)(2,1)S(1)}, u32[]{:S(2)}, u32[]{:S(2)}) collective-permute-start(bf16[2,256,256]{2,1,0:T(8,128)(2,1)S(1)} %fusion.50), channel_id=1, source_target_pairs={{0,2},{2,0},{1,3},{3,1},{4,6},{6,4},{5,7},{7,5},{8,10},{10,8},{9,1... | collective-permute-start | bytes 786440 | tf_op jit(solution)/shard_map/ppermute | solution.py:18
  161.7 1.1 fusion.55
  162.8 0.9 copy.192
  163.7 3.3 %collective-permute-done.14 = bf16[2,256,256]{2,1,0:T(8,128)(2,1)S(1)} collective-permute-done((bf16[2,256,256]{2,1,0:T(8,128)(2,1)S(1)}, bf16[2,256,256]{2,1,0:T(8,128)(2,1)S(1)}, u32[]{:S(2)}, u32[]{:S(2)}) %collective-permute-start.14) | collective-permute-done | bytes 262176 | tf_op jit(solution)/shard_map/ppermute | solution.py:18
  167.1 0.8 collective-permute-start.15
  167.9 14.9 %collective-permute-done.16 = bf16[2,1024,256]{2,1,0:T(8,128)(2,1)S(1)} collective-permute-done((bf16[2,1024,256]{2,1,0:T(8,128)(2,1)S(1)}, bf16[2,1024,256]{2,1,0:T(8,128)(2,1)S(1)}, u32[]{:S(2)}, u32[]{:S(2)}) %collective-permute-start.16) | collective-permute-done | bytes 1048608 | tf_op jit(solution)/shard_map/ppermute | solution.py:18
  185.6 6.9 %collective-permute-done.17 = bf16[2,512,256]{2,1,0:T(8,128)(2,1)S(1)} collective-permute-done((bf16[2,512,256]{2,1,0:T(8,128)(2,1)S(1)}, bf16[2,512,256]{2,1,0:T(8,128)(2,1)S(1)}, u32[]{:S(2)}, u32[]{:S(2)}) %collective-permute-start.17) | collective-permute-done | bytes 524320 | tf_op jit(solution)/shard_map/ppermute | solution.py:18
  193.5 3.5 %collective-permute-start.18 = (bf16[2,256,256]{2,1,0:T(8,128)(2,1)}, bf16[2,256,256]{2,1,0:T(8,128)(2,1)S(1)}, u32[]{:S(2)}, u32[]{:S(2)}) collective-permute-start(bf16[2,256,256]{2,1,0:T(8,128)(2,1)} %fusion.51), channel_id=1, source_target_pairs={{0,2},{2,0},{1,3},{3,1},{4,6},{6,4},{5,7},{7,5},{8,10},{10,8},{9,1... | collective-permute-start | bytes 786440 | tf_op jit(solution)/shard_map/ppermute | solution.py:18
  197.1 1.2 fusion.6
  199.1 63.0 %psum.7 = f32[256]{0:T(256)} all-reduce(f32[256]{0:T(256)S(1)} %bitcast.569), channel_id=1, replica_groups=mesh['dp'=8,'ctx'=16] {'dp','ctx'}, use_global_device_ids=true, to_apply=%region_1.2 | all-reduce | flops 256 | bytes 2048 | tf_op jit(solution)/shard_map/psum | solution.py:217
  262.3 1.5 collective-permute-start.19
  264.4 3.2 %collective-permute-done.19 = bf16[2,128,256]{2,1,0:T(8,128)(2,1)S(1)} collective-permute-done((bf16[2,128,256]{2,1,0:T(8,128)(2,1)S(1)}, bf16[2,128,256]{2,1,0:T(8,128)(2,1)S(1)}, u32[]{:S(2)}, u32[]{:S(2)}) %collective-permute-start.19) | collective-permute-done | bytes 131104 | tf_op jit(solution)/shard_map/ppermute | solution.py:18
  267.9 2.4 fusion.3
  270.7 0.7 convert_element_type.423
  271.5 0.7 convert_element_type.420
  (296 shorter events, 36.4 us)
Async XLA Ops:
  3.4 5.4 %copy-start.28 = (s32[2]{0:T(128)}, s32[2]{0:T(128)S(1)}, u32[]{:S(2)}) copy-start(s32[2]{0:T(128)S(1)} %get-tuple-element.178) | copy-start | bytes 28
  3.4 5.4 %copy-start.30 = (s32[2]{0:T(128)}, s32[2]{0:T(128)S(1)}, u32[]{:S(2)}) copy-start(s32[2]{0:T(128)S(1)} %get-tuple-element.181) | copy-start | bytes 28
  3.4 5.4 %copy-start.32 = (s32[2]{0:T(128)}, s32[2]{0:T(128)S(1)}, u32[]{:S(2)}) copy-start(s32[2]{0:T(128)S(1)} %get-tuple-element.118) | copy-start | bytes 28
  3.4 5.4 %copy-start.34 = (s32[2]{0:T(128)}, s32[2]{0:T(128)S(1)}, u32[]{:S(2)}) copy-start(s32[2]{0:T(128)S(1)} %get-tuple-element.164) | copy-start | bytes 28
  5.4 26.5 %collective-permute-start = (bf16[2,128,256]{2,1,0:T(8,128)(2,1)S(1)}, bf16[2,128,256]{2,1,0:T(8,128)(2,1)S(1)}, u32[]{:S(2)}, u32[]{:S(2)}) collective-permute-start(bf16[2,128,256]{2,1,0:T(8,128)(2,1)S(1)} %bitcast_dynamic-update-slice_fusion.6), channel_id=1, source_target_pairs={{0,1},{1,0},{2,3},{3,2},{4,5},{5,4},{6,7},{7,6},{8,9},{9,8},{10,11... | collective-permute-start | bytes 393224 | tf_op jit(solution)/shard_map/ppermute | solution.py:18
  7.6 5.4 %copy-start.46 = (f32[1,2,256]{2,1,0:T(2,128)S(1)}, f32[1,2,256]{2,1,0:T(2,128)}, u32[]{:S(2)}) copy-start(f32[1,2,256]{2,1,0:T(2,128)} %param.11) | copy-start | bytes 6148
  7.9 26.5 %collective-permute-start.1 = (bf16[2,128,256]{2,1,0:T(8,128)(2,1)S(1)}, bf16[2,128,256]{2,1,0:T(8,128)(2,1)S(1)}, u32[]{:S(2)}, u32[]{:S(2)}) collective-permute-start(bf16[2,128,256]{2,1,0:T(8,128)(2,1)S(1)} %bitcast_dynamic-update-slice_fusion.4), channel_id=1, source_target_pairs={{0,1},{1,0},{2,3},{3,2},{4,5},{5,4},{6,7},{7,6},{8,9},{9,8},{10,11... | collective-permute-start | bytes 393224 | tf_op jit(solution)/shard_map/ppermute | solution.py:18
  8.5 8.3 %copy-start.25 = (bf16[1,256,256]{2,1,0:T(8,128)(2,1)S(1)}, bf16[1,256,256]{2,1,0:T(8,128)(2,1)}, u32[]{:S(2)}) copy-start(bf16[1,256,256]{2,1,0:T(8,128)(2,1)} %param.10) | copy-start | bytes 393220
  9.4 32.7 %collective-permute-start.3 = (bf16[2,128,256]{2,1,0:T(8,128)(2,1)S(1)}, bf16[2,128,256]{2,1,0:T(8,128)(2,1)S(1)}, u32[]{:S(2)}, u32[]{:S(2)}) collective-permute-start(bf16[2,128,256]{2,1,0:T(8,128)(2,1)S(1)} %bitcast_dynamic-update-slice_fusion.2), channel_id=1, source_target_pairs={{0,1},{1,0},{2,3},{3,2},{4,5},{5,4},{6,7},{7,6},{8,9},{9,8},{10,11... | collective-permute-start | bytes 393224 | tf_op jit(solution)/shard_map/ppermute | solution.py:18
  11.9 27.4 %collective-permute-start.6 = (bf16[2,128,256]{2,1,0:T(8,128)(2,1)S(1)}, bf16[2,128,256]{2,1,0:T(8,128)(2,1)S(1)}, u32[]{:S(2)}, u32[]{:S(2)}) collective-permute-start(bf16[2,128,256]{2,1,0:T(8,128)(2,1)S(1)} %bitcast_dynamic-update-slice_fusion), channel_id=1, source_target_pairs={{0,1},{1,0},{2,3},{3,2},{4,5},{5,4},{6,7},{7,6},{8,9},{9,8},{10,11... | collective-permute-start | bytes 393224 | tf_op jit(solution)/shard_map/ppermute | solution.py:18
  13.0 8.2 %copy-start.57 = (s32[2,2]{1,0:T(2,128)}, s32[2,2]{1,0:T(2,128)S(1)}, u32[]{:S(2)}) copy-start(s32[2,2]{1,0:T(2,128)S(1)} %iota_clamp_fusion) | copy-start | bytes 52
  13.0 8.6 %copy-start.51 = (f32[2,2]{1,0:T(2,128)}, f32[2,2]{1,0:T(2,128)S(1)}, u32[]{:S(2)}) copy-start(f32[2,2]{1,0:T(2,128)S(1)} %and_convert_fusion.8) | copy-start | bytes 52
  24.8 5.3 %copy-start.42 = (s32[2,1]{1,0:T(2,128)S(1)}, s32[2,1]{1,0:T(2,128)}, u32[]{:S(2)}) copy-start(s32[2,1]{1,0:T(2,128)} %get-tuple-element.179) | copy-start | bytes 28
  24.8 5.3 %copy-start.43 = (s32[2,1]{1,0:T(2,128)S(1)}, s32[2,1]{1,0:T(2,128)}, u32[]{:S(2)}) copy-start(s32[2,1]{1,0:T(2,128)} %get-tuple-element.180) | copy-start | bytes 28
  24.9 5.5 %copy-start.40 = (s32[2,1]{1,0:T(2,128)S(1)}, s32[2,1]{1,0:T(2,128)}, u32[]{:S(2)}) copy-start(s32[2,1]{1,0:T(2,128)} %get-tuple-element.176) | copy-start | bytes 28
  24.9 5.5 %copy-start.41 = (s32[2,1]{1,0:T(2,128)S(1)}, s32[2,1]{1,0:T(2,128)}, u32[]{:S(2)}) copy-start(s32[2,1]{1,0:T(2,128)} %get-tuple-element.177) | copy-start | bytes 28
  24.9 5.6 %copy-start.38 = (s32[2,1]{1,0:T(2,128)S(1)}, s32[2,1]{1,0:T(2,128)}, u32[]{:S(2)}) copy-start(s32[2,1]{1,0:T(2,128)} %get-tuple-element.119) | copy-start | bytes 28
  24.9 5.6 %copy-start.39 = (s32[2,1]{1,0:T(2,128)S(1)}, s32[2,1]{1,0:T(2,128)}, u32[]{:S(2)}) copy-start(s32[2,1]{1,0:T(2,128)} %get-tuple-element.120) | copy-start | bytes 28
  24.9 5.7 %copy-start.33 = (s32[2]{0:T(128)S(1)}, s32[2]{0:T(128)}, u32[]{:S(2)}) copy-start(s32[2]{0:T(128)} %copy-done.32) | copy-start | bytes 28
  24.9 5.7 %copy-start.35 = (s32[2]{0:T(128)S(1)}, s32[2]{0:T(128)}, u32[]{:S(2)}) copy-start(s32[2]{0:T(128)} %copy-done.34) | copy-start | bytes 28
  24.9 6.3 %copy-start.29 = (s32[2]{0:T(128)S(1)}, s32[2]{0:T(128)}, u32[]{:S(2)}) copy-start(s32[2]{0:T(128)} %copy-done.28) | copy-start | bytes 28
  24.9 6.3 %copy-start.31 = (s32[2]{0:T(128)S(1)}, s32[2]{0:T(128)}, u32[]{:S(2)}) copy-start(s32[2]{0:T(128)} %copy-done.30) | copy-start | bytes 28
  25.3 6.7 %copy-start.62 = (f32[2,1,128]{2,1,0:T(1,128)S(1)}, f32[2,1,128]{2,1,0:T(1,128)}, u32[]{:S(2)}) copy-start(f32[2,1,128]{2,1,0:T(1,128)} %fusion.197) | copy-start | bytes 3076
  33.0 12.7 %copy-start.61 = (f32[2,1,128]{2,1,0:T(1,128)S(1)}, f32[2,1,128]{2,1,0:T(1,128)}, u32[]{:S(2)}) copy-start(f32[2,1,128]{2,1,0:T(1,128)} %fusion.187) | copy-start | bytes 3076
  34.6 10.8 %collective-permute-start.2 = (bf16[2,256,256]{2,1,0:T(8,128)(2,1)S(1)}, bf16[2,256,256]{2,1,0:T(8,128)(2,1)S(1)}, u32[]{:S(2)}, u32[]{:S(2)}) collective-permute-start(bf16[2,256,256]{2,1,0:T(8,128)(2,1)S(1)} %maximum_select_fusion.7), channel_id=1, source_target_pairs={{0,2},{2,0},{1,3},{3,1},{4,6},{6,4},{5,7},{7,5},{8,10},{10,8},{9,1... | collective-permute-start | bytes 786440 | tf_op jit(solution)/shard_map/ppermute | solution.py:18
  38.7 58.8 %collective-permute-start.10 = (bf16[2,128,256]{2,1,0:T(8,128)(2,1)}, bf16[2,128,256]{2,1,0:T(8,128)(2,1)}, u32[]{:S(2)}, u32[]{:S(2)}) collective-permute-start(bf16[2,128,256]{2,1,0:T(8,128)(2,1)} %fusion.67), channel_id=1, source_target_pairs={{0,1},{1,0},{2,3},{3,2},{4,5},{5,4},{6,7},{7,6},{8,9},{9,8},{10,11... | collective-permute-start | bytes 393224 | tf_op jit(solution)/shard_map/ppermute | solution.py:18
  40.1 26.1 %collective-permute-start.7 = (bf16[2,256,256]{2,1,0:T(8,128)(2,1)}, bf16[2,256,256]{2,1,0:T(8,128)(2,1)}, u32[]{:S(2)}, u32[]{:S(2)}) collective-permute-start(bf16[2,256,256]{2,1,0:T(8,128)(2,1)} %maximum_select_fusion.9), channel_id=1, source_target_pairs={{0,2},{2,0},{1,3},{3,1},{4,6},{6,4},{5,7},{7,5},{8,10},{10,8},{9,1... | collective-permute-start | bytes 786440 | tf_op jit(solution)/shard_map/ppermute | solution.py:18
  42.9 14.2 %collective-permute-start.4 = (bf16[2,256,256]{2,1,0:T(8,128)(2,1)}, bf16[2,256,256]{2,1,0:T(8,128)(2,1)}, u32[]{:S(2)}, u32[]{:S(2)}) collective-permute-start(bf16[2,256,256]{2,1,0:T(8,128)(2,1)} %maximum_select_fusion.8), channel_id=1, source_target_pairs={{0,2},{2,0},{1,3},{3,1},{4,6},{6,4},{5,7},{7,5},{8,10},{10,8},{9,1... | collective-permute-start | bytes 786440 | tf_op jit(solution)/shard_map/ppermute | solution.py:18
  58.4 14.8 %collective-permute-start.5 = (bf16[2,512,256]{2,1,0:T(8,128)(2,1)S(1)}, bf16[2,512,256]{2,1,0:T(8,128)(2,1)}, u32[]{:S(2)}, u32[]{:S(2)}) collective-permute-start(bf16[2,512,256]{2,1,0:T(8,128)(2,1)S(1)} %maximum_select_fusion.4), channel_id=1, source_target_pairs={{0,4},{4,0},{1,5},{5,1},{2,6},{6,2},{3,7},{7,3},{8,12},{12,8},{9,1... | collective-permute-start | bytes 1572872 | tf_op jit(solution)/shard_map/ppermute | solution.py:18
  62.3 12.3 %copy-start.19 = (bf16[2,1,16384]{2,0,1:T(2,128)(2,1)S(1)}, bf16[2,1,16384]{2,0,1:T(2,128)(2,1)}, u32[]{:S(2)}) copy-start(bf16[2,1,16384]{2,0,1:T(2,128)(2,1)} %copy.384) | copy-start | bytes 196612
  62.3 12.3 %copy-start.27 = (f32[1,2,8,128]{3,1,2,0:T(2,128)S(1)}, f32[1,2,8,128]{3,1,2,0:T(2,128)}, u32[]{:S(2)}) copy-start(f32[1,2,8,128]{3,1,2,0:T(2,128)} %copy.393) | copy-start | bytes 24580
  62.3 12.3 %copy-start.50 = (f32[2]{0:T(128)S(1)}, f32[2]{0:T(128)}, u32[]{:S(2)}) copy-start(f32[2]{0:T(128)} %copy-done.49) | copy-start | bytes 28
  62.4 12.3 %copy-start.60 = (f32[2,1,128]{2,1,0:T(1,128)S(1)}, f32[2,1,128]{2,1,0:T(1,128)}, u32[]{:S(2)}) copy-start(f32[2,1,128]{2,1,0:T(1,128)} %fusion.177) | copy-start | bytes 3076
  63.1 36.2 %collective-permute-start.11 = (bf16[2,256,256]{2,1,0:T(8,128)(2,1)}, bf16[2,256,256]{2,1,0:T(8,128)(2,1)}, u32[]{:S(2)}, u32[]{:S(2)}) collective-permute-start(bf16[2,256,256]{2,1,0:T(8,128)(2,1)} %fusion.49), channel_id=1, source_target_pairs={{0,2},{2,0},{1,3},{3,1},{4,6},{6,4},{5,7},{7,5},{8,10},{10,8},{9,1... | collective-permute-start | bytes 786440 | tf_op jit(solution)/shard_map/ppermute | solution.py:18
  68.3 23.8 %collective-permute-start.8 = (bf16[2,512,256]{2,1,0:T(8,128)(2,1)}, bf16[2,512,256]{2,1,0:T(8,128)(2,1)}, u32[]{:S(2)}, u32[]{:S(2)}) collective-permute-start(bf16[2,512,256]{2,1,0:T(8,128)(2,1)} %maximum_select_fusion.5), channel_id=1, source_target_pairs={{0,4},{4,0},{1,5},{5,1},{2,6},{6,2},{3,7},{7,3},{8,12},{12,8},{9,1... | collective-permute-start | bytes 1572872 | tf_op jit(solution)/shard_map/ppermute | solution.py:18
  89.2 8.3 %copy-start.6 = (f32[2,256,256]{2,1,0:T(8,128)S(1)}, f32[2,256,256]{2,1,0:T(8,128)}, u32[]{:S(2)}) copy-start(f32[2,256,256]{2,1,0:T(8,128)} %copy-done.5) | copy-start | bytes 1572868
  89.4 15.5 %collective-permute-start.13 = (bf16[2,512,256]{2,1,0:T(8,128)(2,1)S(1)}, bf16[2,512,256]{2,1,0:T(8,128)(2,1)S(1)}, u32[]{:S(2)}, u32[]{:S(2)}) collective-permute-start(bf16[2,512,256]{2,1,0:T(8,128)(2,1)S(1)} %fusion.42), channel_id=1, source_target_pairs={{0,4},{4,0},{1,5},{5,1},{2,6},{6,2},{3,7},{7,3},{8,12},{12,8},{9,1... | collective-permute-start | bytes 1572872 | tf_op jit(solution)/shard_map/ppermute | solution.py:18
  93.8 29.7 %collective-permute-start.9 = (bf16[2,1024,256]{2,1,0:T(8,128)(2,1)S(1)}, bf16[2,1024,256]{2,1,0:T(8,128)(2,1)S(1)}, u32[]{:S(2)}, u32[]{:S(2)}) collective-permute-start(bf16[2,1024,256]{2,1,0:T(8,128)(2,1)S(1)} %maximum_select_fusion.2), channel_id=1, source_target_pairs={{0,8},{8,0},{1,9},{9,1},{2,10},{10,2},{3,11},{11,3},{4,12},{12,4},... | collective-permute-start | bytes 3145736 | tf_op jit(solution)/shard_map/ppermute | solution.py:18
  101.1 60.6 %collective-permute-start.12 = (bf16[2,128,256]{2,1,0:T(8,128)(2,1)}, bf16[2,128,256]{2,1,0:T(8,128)(2,1)}, u32[]{:S(2)}, u32[]{:S(2)}) collective-permute-start(bf16[2,128,256]{2,1,0:T(8,128)(2,1)} %fusion.68), channel_id=1, source_target_pairs={{0,1},{1,0},{2,3},{3,2},{4,5},{5,4},{6,7},{7,6},{8,9},{9,8},{10,11... | collective-permute-start | bytes 393224 | tf_op jit(solution)/shard_map/ppermute | solution.py:18
  105.1 19.0 %copy-start.18 = (bf16[2,1,16384]{2,0,1:T(2,128)(2,1)S(1)}, bf16[2,1,16384]{2,0,1:T(2,128)(2,1)}, u32[]{:S(2)}) copy-start(bf16[2,1,16384]{2,0,1:T(2,128)(2,1)} %copy.388) | copy-start | bytes 196612
  105.1 19.0 %copy-start.48 = (f32[2]{0:T(128)S(1)}, f32[2]{0:T(128)}, u32[]{:S(2)}) copy-start(f32[2]{0:T(128)} %copy-done.47) | copy-start | bytes 28
  105.2 19.0 %copy-start.59 = (f32[2,1,128]{2,1,0:T(1,128)S(1)}, f32[2,1,128]{2,1,0:T(1,128)}, u32[]{:S(2)}) copy-start(f32[2,1,128]{2,1,0:T(1,128)} %fusion.167) | copy-start | bytes 3076
  156.2 5.5 %copy-start.8 = (f32[2,256,256]{2,1,0:T(8,128)S(1)}, f32[2,256,256]{2,1,0:T(8,128)}, u32[]{:S(2)}) copy-start(f32[2,256,256]{2,1,0:T(8,128)} %copy-done.7) | copy-start | bytes 1572868
  158.1 24.7 %collective-permute-start.16 = (bf16[2,1024,256]{2,1,0:T(8,128)(2,1)S(1)}, bf16[2,1024,256]{2,1,0:T(8,128)(2,1)S(1)}, u32[]{:S(2)}, u32[]{:S(2)}) collective-permute-start(bf16[2,1024,256]{2,1,0:T(8,128)(2,1)S(1)} %fusion.36), channel_id=1, source_target_pairs={{0,8},{8,0},{1,9},{9,1},{2,10},{10,2},{3,11},{11,3},{4,12},{12,4},... | collective-permute-start | bytes 3145736 | tf_op jit(solution)/shard_map/ppermute | solution.py:18
  158.3 8.7 %collective-permute-start.14 = (bf16[2,256,256]{2,1,0:T(8,128)(2,1)S(1)}, bf16[2,256,256]{2,1,0:T(8,128)(2,1)S(1)}, u32[]{:S(2)}, u32[]{:S(2)}) collective-permute-start(bf16[2,256,256]{2,1,0:T(8,128)(2,1)S(1)} %fusion.50), channel_id=1, source_target_pairs={{0,2},{2,0},{1,3},{3,1},{4,6},{6,4},{5,7},{7,5},{8,10},{10,8},{9,1... | collective-permute-start | bytes 786440 | tf_op jit(solution)/shard_map/ppermute | solution.py:18
  161.6 21.2 %copy-start = (f32[2,1,1024,256]{3,2,0,1:T(8,128)S(1)}, f32[2,1,1024,256]{3,2,0,1:T(8,128)}, u32[]{:S(2)}) copy-start(f32[2,1,1024,256]{3,2,0,1:T(8,128)} %copy.158) | copy-start | bytes 6291460
  167.1 16.3 %copy-start.12 = (bf16[2,1024,256]{2,1,0:T(8,128)(2,1)S(1)}, bf16[2,1024,256]{2,1,0:T(8,128)(2,1)}, u32[]{:S(2)}) copy-start(bf16[2,1024,256]{2,1,0:T(8,128)(2,1)} %copy-done.11) | copy-start | bytes 3145732
  167.1 16.3 %copy-start.16 = (bf16[2,128,1024]{2,1,0:T(8,128)(2,1)S(1)}, bf16[2,128,1024]{2,1,0:T(8,128)(2,1)}, u32[]{:S(2)}) copy-start(bf16[2,128,1024]{2,1,0:T(8,128)(2,1)} %copy-done.15) | copy-start | bytes 1572868
  167.1 16.7 %collective-permute-start.15 = (bf16[2,128,256]{2,1,0:T(8,128)(2,1)S(1)}, bf16[2,128,256]{2,1,0:T(8,128)(2,1)S(1)}, u32[]{:S(2)}, u32[]{:S(2)}) collective-permute-start(bf16[2,128,256]{2,1,0:T(8,128)(2,1)S(1)} %fusion.69), channel_id=1, source_target_pairs={{0,1},{1,0},{2,3},{3,2},{4,5},{5,4},{6,7},{7,6},{8,9},{9,8},{10,11... | collective-permute-start | bytes 393224 | tf_op jit(solution)/shard_map/ppermute | solution.py:18
  183.3 9.3 %collective-permute-start.17 = (bf16[2,512,256]{2,1,0:T(8,128)(2,1)S(1)}, bf16[2,512,256]{2,1,0:T(8,128)(2,1)S(1)}, u32[]{:S(2)}, u32[]{:S(2)}) collective-permute-start(bf16[2,512,256]{2,1,0:T(8,128)(2,1)S(1)} %fusion.43), channel_id=1, source_target_pairs={{0,4},{4,0},{1,5},{5,1},{2,6},{6,2},{3,7},{7,3},{8,12},{12,8},{9,1... | collective-permute-start | bytes 1572872 | tf_op jit(solution)/shard_map/ppermute | solution.py:18
  185.6 11.5 %copy-start.20 = (f32[2,2,16384]{2,1,0:T(2,128)S(1)}, f32[2,2,16384]{2,1,0:T(2,128)}, u32[]{:S(2)}) copy-start(f32[2,2,16384]{2,1,0:T(2,128)} %reshape_reshape_transpose.2) | copy-start | bytes 786436
  185.6 11.5 %copy-start.26 = (f32[1,2,128,128]{3,1,2,0:T(2,128)S(1)}, f32[1,2,128,128]{3,1,2,0:T(2,128)}, u32[]{:S(2)}) copy-start(f32[1,2,128,128]{3,1,2,0:T(2,128)} %copy.373) | copy-start | bytes 393220
  185.6 11.4 %copy-start.52 = (f32[2,2]{1,0:T(2,128)S(1)}, f32[2,2]{1,0:T(2,128)}, u32[]{:S(2)}) copy-start(f32[2,2]{1,0:T(2,128)} %copy-done.51) | copy-start | bytes 52
  185.6 11.4 %copy-start.53 = (f32[2,2]{1,0:T(2,128)S(1)}, f32[2,2]{1,0:T(2,128)}, u32[]{:S(2)}) copy-start(f32[2,2]{1,0:T(2,128)} %get-tuple-element.207) | copy-start | bytes 52
  185.6 11.4 %copy-start.54 = (f32[2,2]{1,0:T(2,128)S(1)}, f32[2,2]{1,0:T(2,128)}, u32[]{:S(2)}) copy-start(f32[2,2]{1,0:T(2,128)} %get-tuple-element.208) | copy-start | bytes 52
  185.6 11.4 %copy-start.55 = (f32[2,2]{1,0:T(2,128)S(1)}, f32[2,2]{1,0:T(2,128)}, u32[]{:S(2)}) copy-start(f32[2,2]{1,0:T(2,128)} %get-tuple-element.203) | copy-start | bytes 52
  185.6 11.4 %copy-start.56 = (f32[2,2]{1,0:T(2,128)S(1)}, f32[2,2]{1,0:T(2,128)}, u32[]{:S(2)}) copy-start(f32[2,2]{1,0:T(2,128)} %get-tuple-element.204) | copy-start | bytes 52
  185.6 11.4 %copy-start.58 = (s32[2,2]{1,0:T(2,128)S(1)}, s32[2,2]{1,0:T(2,128)}, u32[]{:S(2)}) copy-start(s32[2,2]{1,0:T(2,128)} %copy-done.57) | copy-start | bytes 52
  193.5 68.7 %collective-permute-start.18 = (bf16[2,256,256]{2,1,0:T(8,128)(2,1)}, bf16[2,256,256]{2,1,0:T(8,128)(2,1)S(1)}, u32[]{:S(2)}, u32[]{:S(2)}) collective-permute-start(bf16[2,256,256]{2,1,0:T(8,128)(2,1)} %fusion.51), channel_id=1, source_target_pairs={{0,2},{2,0},{1,3},{3,1},{4,6},{6,4},{5,7},{7,5},{8,10},{10,8},{9,1... | collective-permute-start | bytes 786440 | tf_op jit(solution)/shard_map/ppermute | solution.py:18
  198.3 65.4 %copy-start.37 = (f32[256]{0:T(256)S(1)}, f32[256]{0:T(256)}, u32[]{:S(2)}) copy-start(f32[256]{0:T(256)} %param.13) | copy-start | bytes 3076
  199.1 68.8 %copy-start.17 = (f32[2,2,32768]{2,1,0:T(2,128)S(1)}, f32[2,2,32768]{2,1,0:T(2,128)}, u32[]{:S(2)}) copy-start(f32[2,2,32768]{2,1,0:T(2,128)} %reshape.1667) | copy-start | bytes 1572868
  199.1 68.8 %copy-start.21 = (f32[1,2,128,256]{3,1,2,0:T(2,128)S(1)}, f32[1,2,128,256]{3,1,2,0:T(2,128)}, u32[]{:S(2)}) copy-start(f32[1,2,128,256]{3,1,2,0:T(2,128)} %copy.191) | copy-start | bytes 786436
  199.1 68.8 %copy-start.22 = (f32[1,2,128,256]{3,1,2,0:T(2,128)S(1)}, f32[1,2,128,256]{3,1,2,0:T(2,128)}, u32[]{:S(2)}) copy-start(f32[1,2,128,256]{3,1,2,0:T(2,128)} %copy.192) | copy-start | bytes 786436
  262.3 5.3 %collective-permute-start.19 = (bf16[2,128,256]{2,1,0:T(8,128)(2,1)S(1)}, bf16[2,128,256]{2,1,0:T(8,128)(2,1)S(1)}, u32[]{:S(2)}, u32[]{:S(2)}) collective-permute-start(bf16[2,128,256]{2,1,0:T(8,128)(2,1)S(1)} %fusion.70), channel_id=1, source_target_pairs={{0,1},{1,0},{2,3},{3,2},{4,5},{5,4},{6,7},{7,6},{8,9},{9,8},{10,11... | collective-permute-start | bytes 393224 | tf_op jit(solution)/shard_map/ppermute | solution.py:18
  (19 other events, 51.9 us)
where the time goes:
time: 277 us; the launch traced here: 273 us
  waiting for transfers between devices  63.6 us (23%)
  blocking collectives  63 us (23%)
  local copies, waits for them, and re-layouts  59.3 us (21%)
  starting transfers between devices  34.9 us (13%)
  other arithmetic  27.5 us (10%)
  matrix products  21.6 us (8%)
    ppermute x20, waiting for transfers between devices, swapped(): return lax.ppermute(block, axis, route)  63.6 us
    psum x1, blocking collectives, body(): lax.psum(jnp.sum(query_raw.astype(jnp.float32) * dq_rows, axis=0), ('dp',...  63 us
    ppermute x20, starting transfers between devices, swapped(): return lax.ppermute(block, axis, route)  34.9 us
    unnamed x153, local copies, waits for them, and re-layouts  24.8 us
    slice x3, local copies, waits for them, and re-layouts, swap_down(): kept_half = jnp.where(lower_half, halves[:, 0], halves[:, 1])  12.9 us
    reshape x3, local copies, waits for them, and re-layouts, swap_down(): halves = sums_kv.reshape(head_count, 2, -1, sums_kv.shape[-1])  10.3 us
    dot_general x25, matrix products, pick_blocks(): jnp.einsum('hsb,hbx->hsx', table, flat, precision=lax.Precision.HIGHEST,...  10.3 us
    select_n x10, other arithmetic, swap_up(): jnp.where(lower_half, jnp.concatenate([payload, partner], axis=1), jnp.co...  9.27 us
  transfers between devices with their start and end apart: 20, of which 9 were waited for; matrix products, arithmetic and copies ran while one was open for 34% of the time, Pallas kernels for 0%

commit v1 on v0

--- a/solution.py
+++ b/solution.py
@@ -214,7 +214,9 @@
     grad_queries = (dq_rows * q_gain).astype(jnp.bfloat16)
     grad_keys = to_rows(kv_acc[..., :head_dim]).astype(jnp.bfloat16)
     grad_values = to_rows(kv_acc[..., head_dim:]).astype(jnp.bfloat16)
-    gain_total = lax.psum(jnp.sum(query_raw.astype(jnp.float32) * dq_rows, axis=0), ("dp", "ctx"))
+    gain_total = lax.psum(
+        lax.psum(jnp.sum(query_raw.astype(jnp.float32) * dq_rows, axis=0), "dp"), "ctx"
+    )
     return (grad_queries[None], grad_keys[None], grad_values[None], gain_total)
 
 

time: 277 us -> 263 us (0.949)
  blocking collectives: 63 us -> 49.3 us
    psum x1 -> x2, blocking collectives: 63 us -> 49.3 us  [the longest x1 36.7 us: body(): lax.psum(lax.psum(jnp.sum(query_raw.astype(jnp.float32) * dq_rows, axis=0...]
  transfers between devices with their start and end apart: 20 -> 20, of which waited for: 9 -> 9; matrix products, arithmetic and copies ran while one was open for 34% -> 36% of each run, Pallas kernels for 0% -> 0%
where the time goes in v1:
time: 263 us; the launch traced here: 259 us
  waiting for transfers between devices  63.2 us (24%)
  local copies, waits for them, and re-layouts  58.9 us (22%)
  blocking collectives  49.3 us (19%)
  starting transfers between devices  35.4 us (13%)
  other arithmetic  27.6 us (10%)
  matrix products  21.7 us (8%)
    ppermute x20, waiting for transfers between devices, swapped(): return lax.ppermute(block, axis, route)  63.2 us
    psum x1, blocking collectives, body(): lax.psum(lax.psum(jnp.sum(query_raw.astype(jnp.float32) * dq_rows, axis=0...  36.7 us
    ppermute x20, starting transfers between devices, swapped(): return lax.ppermute(block, axis, route)  35.4 us
    unnamed x153, local copies, waits for them, and re-layouts  24.5 us
    slice x3, local copies, waits for them, and re-layouts, swap_down(): kept_half = jnp.where(lower_half, halves[:, 0], halves[:, 1])  12.9 us
    psum x1, blocking collectives, body(): lax.psum(jnp.sum(query_raw.astype(jnp.float32) * dq_rows, axis=0), 'dp')  12.6 us
    dot_general x25, matrix products, pick_blocks(): jnp.einsum('hsb,hbx->hsx', table, flat, precision=lax.Precision.HIGHEST,...  10.3 us
    reshape x3, local copies, waits for them, and re-layouts, swap_down(): halves = sums_kv.reshape(head_count, 2, -1, sums_kv.shape[-1])  10.3 us
  transfers between devices with their start and end apart: 20, of which 9 were waited for; matrix products, arithmetic and copies ran while one was open for 36% of the time, Pallas kernels for 0%

profile of v1, /device:TPU:0, one launch (start us, length us, event | category | flops | bytes accessed | tf_op | source)
XLA Modules:
  0.0 258.7 jit_solution(1549517799884695533)
XLA Ops:
  0.7 0.9 reshape_squeeze.12
  1.7 1.7 clamp_reduce_fusion.3
  4.0 0.9 reshape_squeeze.15
  5.4 1.7 collective-permute-start
  9.4 1.7 collective-permute-start.3
  11.9 1.1 collective-permute-start.6
  19.4 0.9 fusion.193
  20.4 0.9 fusion.203
  26.9 1.0 copy.380
  28.1 0.9 reshape_reshape_transpose.2
  29.0 1.2 reshape.1667
  33.1 0.8 copy-done.5
  34.7 3.2 %collective-permute-start.2 = (bf16[2,256,256]{2,1,0:T(8,128)(2,1)S(1)}, bf16[2,256,256]{2,1,0:T(8,128)(2,1)S(1)}, u32[]{:S(2)}, u32[]{:S(2)}) collective-permute-start(bf16[2,256,256]{2,1,0:T(8,128)(2,1)S(1)} %maximum_select_fusion.7), channel_id=1, source_target_pairs={{0,2},{2,0},{1,3},{3,1},{4,6},{6,4},{5,7},{7,5},{8,10},{10,8},{9,1... | collective-permute-start | bytes 786440 | tf_op jit(solution)/shard_map/ppermute | solution.py:18
  38.1 0.8 copy.373
  39.5 0.8 maximum_select_fusion.9
  40.3 2.0 collective-permute-start.7
  42.3 0.8 maximum_select_fusion.8
  43.1 1.5 collective-permute-start.4
  44.6 1.0 collective-permute-done.2
  48.1 9.2 %collective-permute-done.4 = bf16[2,256,256]{2,1,0:T(8,128)(2,1)} collective-permute-done((bf16[2,256,256]{2,1,0:T(8,128)(2,1)}, bf16[2,256,256]{2,1,0:T(8,128)(2,1)}, u32[]{:S(2)}, u32[]{:S(2)}) %collective-permute-start.4) | collective-permute-done | bytes 262176 | tf_op jit(solution)/shard_map/ppermute | solution.py:18
  57.3 1.3 maximum_select_fusion.4
  58.6 2.4 collective-permute-start.5
  61.0 0.8 fusion.213
  62.5 0.8 fusion.49
  63.3 3.0 %collective-permute-start.11 = (bf16[2,256,256]{2,1,0:T(8,128)(2,1)}, bf16[2,256,256]{2,1,0:T(8,128)(2,1)}, u32[]{:S(2)}, u32[]{:S(2)}) collective-permute-start(bf16[2,256,256]{2,1,0:T(8,128)(2,1)} %fusion.49), channel_id=1, source_target_pairs={{0,2},{2,0},{1,3},{3,1},{4,6},{6,4},{5,7},{7,5},{8,10},{10,8},{9,1... | collective-permute-start | bytes 786440 | tf_op jit(solution)/shard_map/ppermute | solution.py:18
  66.3 2.1 maximum_select_fusion.5
  68.6 4.8 %collective-permute-done.5 = bf16[2,512,256]{2,1,0:T(8,128)(2,1)} collective-permute-done((bf16[2,512,256]{2,1,0:T(8,128)(2,1)S(1)}, bf16[2,512,256]{2,1,0:T(8,128)(2,1)}, u32[]{:S(2)}, u32[]{:S(2)}) %collective-permute-start.5) | collective-permute-done | bytes 524320 | tf_op jit(solution)/shard_map/ppermute | solution.py:18
  73.3 1.4 maximum_select_fusion.1
  77.2 1.5 pad_maximum_fusion.1
  78.7 3.0 %reshape.1673 = f32[2,2,512,256]{2,1,3,0:T(2,128)S(1)} reshape(f32[2,1024,256]{1,2,0:T(8,128)} %pad_maximum_fusion.1) | data formatting | bytes 4194304 | tf_op jit(solution)/shard_map/reshape | solution.py:137
  81.7 3.0 %fusion.212 = (f32[2,1,512,256]{2,1,3,0:T(1,128)}, f32[2,1,512,256]{2,1,3,0:T(1,128)}) fusion(f32[2,2,512,256]{2,1,3,0:T(2,128)S(1)} %reshape.1673), kind=kLoop, calls=%fused_computation.413 | loop fusion | bytes 4194304 | tf_op jit(solution)/shard_map/slice | solution.py:139
  84.7 2.3 copy.151
  87.1 2.4 copy.152
  89.6 2.7 %collective-permute-start.13 = (bf16[2,512,256]{2,1,0:T(8,128)(2,1)S(1)}, bf16[2,512,256]{2,1,0:T(8,128)(2,1)S(1)}, u32[]{:S(2)}, u32[]{:S(2)}) collective-permute-start(bf16[2,512,256]{2,1,0:T(8,128)(2,1)S(1)} %fusion.42), channel_id=1, source_target_pairs={{0,4},{4,0},{1,5},{5,1},{2,6},{6,2},{3,7},{7,3},{8,12},{12,8},{9,1... | collective-permute-start | bytes 1572872 | tf_op jit(solution)/shard_map/ppermute | solution.py:18
  92.3 1.8 maximum_select_fusion.2
  94.0 3.7 %collective-permute-start.9 = (bf16[2,1024,256]{2,1,0:T(8,128)(2,1)S(1)}, bf16[2,1024,256]{2,1,0:T(8,128)(2,1)S(1)}, u32[]{:S(2)}, u32[]{:S(2)}) collective-permute-start(bf16[2,1024,256]{2,1,0:T(8,128)(2,1)S(1)} %maximum_select_fusion.2), channel_id=1, source_target_pairs={{0,8},{8,0},{1,9},{9,1},{2,10},{10,2},{3,11},{11,3},{4,12},{12,4},... | collective-permute-start | bytes 3145736 | tf_op jit(solution)/shard_map/ppermute | solution.py:18
  97.7 1.0 fusion.58
  98.7 0.9 copy.191
  99.6 1.0 bitcast_add_fusion.5
  100.6 0.8 fusion.68
  101.4 1.7 collective-permute-start.12
  103.1 2.0 collective-permute-done.13
  105.4 18.4 %collective-permute-done.9 = bf16[2,1024,256]{2,1,0:T(8,128)(2,1)S(1)} collective-permute-done((bf16[2,1024,256]{2,1,0:T(8,128)(2,1)S(1)}, bf16[2,1024,256]{2,1,0:T(8,128)(2,1)S(1)}, u32[]{:S(2)}, u32[]{:S(2)}) %collective-permute-start.9) | collective-permute-done | bytes 1048608 | tf_op jit(solution)/shard_map/ppermute | solution.py:18
  127.6 2.5 pad_maximum_fusion
  130.1 6.6 %reshape.1677 = f32[2,2,1024,256]{2,1,3,0:T(2,128)} reshape(f32[2,2048,256]{1,2,0:T(8,128)} %pad_maximum_fusion) | data formatting | bytes 8388608 | tf_op jit(solution)/shard_map/reshape | solution.py:137
  136.7 9.1 %fusion.211 = (f32[2,1,1024,256]{2,1,3,0:T(1,128)}, f32[2,1,1024,256]{2,1,3,0:T(1,128)}) fusion(f32[2,2,1024,256]{2,1,3,0:T(2,128)} %reshape.1677), kind=kLoop, calls=%fused_computation.412 | loop fusion | bytes 8388608 | tf_op jit(solution)/shard_map/slice | solution.py:139
  145.8 4.6 %copy.157 = f32[2,1,1024,256]{3,2,0,1:T(8,128)S(1)} copy(f32[2,1,1024,256]{2,1,3,0:T(1,128)} %get-tuple-element.141) | data formatting | bytes 4194304
  150.4 6.1 %copy.158 = f32[2,1,1024,256]{3,2,0,1:T(8,128)} copy(f32[2,1,1024,256]{2,1,3,0:T(1,128)} %get-tuple-element.142) | data formatting | bytes 4194304
  156.4 1.9 fusion.36
  158.5 3.1 %collective-permute-start.14 = (bf16[2,256,256]{2,1,0:T(8,128)(2,1)S(1)}, bf16[2,256,256]{2,1,0:T(8,128)(2,1)S(1)}, u32[]{:S(2)}, u32[]{:S(2)}) collective-permute-start(bf16[2,256,256]{2,1,0:T(8,128)(2,1)S(1)} %fusion.50), channel_id=1, source_target_pairs={{0,2},{2,0},{1,3},{3,1},{4,6},{6,4},{5,7},{7,5},{8,10},{10,8},{9,1... | collective-permute-start | bytes 786440 | tf_op jit(solution)/shard_map/ppermute | solution.py:18
  162.0 1.1 fusion.55
  163.0 0.9 copy.192
  164.0 3.3 %collective-permute-done.14 = bf16[2,256,256]{2,1,0:T(8,128)(2,1)S(1)} collective-permute-done((bf16[2,256,256]{2,1,0:T(8,128)(2,1)S(1)}, bf16[2,256,256]{2,1,0:T(8,128)(2,1)S(1)}, u32[]{:S(2)}, u32[]{:S(2)}) %collective-permute-start.14) | collective-permute-done | bytes 262176 | tf_op jit(solution)/shard_map/ppermute | solution.py:18
  167.4 0.8 collective-permute-start.15
  168.2 14.6 %collective-permute-done.16 = bf16[2,1024,256]{2,1,0:T(8,128)(2,1)S(1)} collective-permute-done((bf16[2,1024,256]{2,1,0:T(8,128)(2,1)S(1)}, bf16[2,1024,256]{2,1,0:T(8,128)(2,1)S(1)}, u32[]{:S(2)}, u32[]{:S(2)}) %collective-permute-start.16) | collective-permute-done | bytes 1048608 | tf_op jit(solution)/shard_map/ppermute | solution.py:18
  185.7 6.9 %collective-permute-done.17 = bf16[2,512,256]{2,1,0:T(8,128)(2,1)S(1)} collective-permute-done((bf16[2,512,256]{2,1,0:T(8,128)(2,1)S(1)}, bf16[2,512,256]{2,1,0:T(8,128)(2,1)S(1)}, u32[]{:S(2)}, u32[]{:S(2)}) %collective-permute-start.17) | collective-permute-done | bytes 524320 | tf_op jit(solution)/shard_map/ppermute | solution.py:18
  192.8 0.7 fusion.51
  193.5 3.8 %collective-permute-start.18 = (bf16[2,256,256]{2,1,0:T(8,128)(2,1)}, bf16[2,256,256]{2,1,0:T(8,128)(2,1)S(1)}, u32[]{:S(2)}, u32[]{:S(2)}) collective-permute-start(bf16[2,256,256]{2,1,0:T(8,128)(2,1)} %fusion.51), channel_id=1, source_target_pairs={{0,2},{2,0},{1,3},{3,1},{4,6},{6,4},{5,7},{7,5},{8,10},{10,8},{9,1... | collective-permute-start | bytes 786440 | tf_op jit(solution)/shard_map/ppermute | solution.py:18
  197.3 1.2 fusion.6
  199.4 12.6 %psum.14 = f32[256]{0:T(256)S(1)} all-reduce(f32[256]{0:T(256)S(1)} %bitcast.569), channel_id=1, replica_groups=mesh['dp'=8,'ctx'=16] {'dp'}, use_global_device_ids=true, to_apply=%region_1.2 | all-reduce | flops 256 | bytes 2048 | tf_op jit(solution)/shard_map/psum | solution.py:218
  211.9 36.7 %psum.15 = f32[256]{0:T(256)} all-reduce(f32[256]{0:T(256)S(1)} %psum.14), channel_id=1, replica_groups=mesh['dp'=8,'ctx'=16] {'ctx'}, use_global_device_ids=true, to_apply=%region_2.3 | all-reduce | flops 256 | bytes 2048 | tf_op jit(solution)/shard_map/psum | solution.py:217
  248.8 1.4 collective-permute-start.19
  250.8 3.0 %collective-permute-done.19 = bf16[2,128,256]{2,1,0:T(8,128)(2,1)S(1)} collective-permute-done((bf16[2,128,256]{2,1,0:T(8,128)(2,1)S(1)}, bf16[2,128,256]{2,1,0:T(8,128)(2,1)S(1)}, u32[]{:S(2)}, u32[]{:S(2)}) %collective-permute-start.19) | collective-permute-done | bytes 131104 | tf_op jit(solution)/shard_map/ppermute | solution.py:18
  254.1 2.4 fusion.3
  (297 shorter events, 37.3 us)
Async XLA Ops:
  3.4 5.4 %copy-start.28 = (s32[2]{0:T(128)}, s32[2]{0:T(128)S(1)}, u32[]{:S(2)}) copy-start(s32[2]{0:T(128)S(1)} %get-tuple-element.178) | copy-start | bytes 28
  3.4 5.4 %copy-start.30 = (s32[2]{0:T(128)}, s32[2]{0:T(128)S(1)}, u32[]{:S(2)}) copy-start(s32[2]{0:T(128)S(1)} %get-tuple-element.181) | copy-start | bytes 28
  3.4 5.4 %copy-start.32 = (s32[2]{0:T(128)}, s32[2]{0:T(128)S(1)}, u32[]{:S(2)}) copy-start(s32[2]{0:T(128)S(1)} %get-tuple-element.118) | copy-start | bytes 28
  3.4 5.4 %copy-start.34 = (s32[2]{0:T(128)}, s32[2]{0:T(128)S(1)}, u32[]{:S(2)}) copy-start(s32[2]{0:T(128)S(1)} %get-tuple-element.164) | copy-start | bytes 28
  5.4 26.6 %collective-permute-start = (bf16[2,128,256]{2,1,0:T(8,128)(2,1)S(1)}, bf16[2,128,256]{2,1,0:T(8,128)(2,1)S(1)}, u32[]{:S(2)}, u32[]{:S(2)}) collective-permute-start(bf16[2,128,256]{2,1,0:T(8,128)(2,1)S(1)} %bitcast_dynamic-update-slice_fusion.6), channel_id=1, source_target_pairs={{0,1},{1,0},{2,3},{3,2},{4,5},{5,4},{6,7},{7,6},{8,9},{9,8},{10,11... | collective-permute-start | bytes 393224 | tf_op jit(solution)/shard_map/ppermute | solution.py:18
  7.6 5.4 %copy-start.46 = (f32[1,2,256]{2,1,0:T(2,128)S(1)}, f32[1,2,256]{2,1,0:T(2,128)}, u32[]{:S(2)}) copy-start(f32[1,2,256]{2,1,0:T(2,128)} %param.11) | copy-start | bytes 6148
  7.9 26.7 %collective-permute-start.1 = (bf16[2,128,256]{2,1,0:T(8,128)(2,1)S(1)}, bf16[2,128,256]{2,1,0:T(8,128)(2,1)S(1)}, u32[]{:S(2)}, u32[]{:S(2)}) collective-permute-start(bf16[2,128,256]{2,1,0:T(8,128)(2,1)S(1)} %bitcast_dynamic-update-slice_fusion.4), channel_id=1, source_target_pairs={{0,1},{1,0},{2,3},{3,2},{4,5},{5,4},{6,7},{7,6},{8,9},{9,8},{10,11... | collective-permute-start | bytes 393224 | tf_op jit(solution)/shard_map/ppermute | solution.py:18
  8.5 8.4 %copy-start.25 = (bf16[1,256,256]{2,1,0:T(8,128)(2,1)S(1)}, bf16[1,256,256]{2,1,0:T(8,128)(2,1)}, u32[]{:S(2)}) copy-start(bf16[1,256,256]{2,1,0:T(8,128)(2,1)} %param.10) | copy-start | bytes 393220
  9.4 32.8 %collective-permute-start.3 = (bf16[2,128,256]{2,1,0:T(8,128)(2,1)S(1)}, bf16[2,128,256]{2,1,0:T(8,128)(2,1)S(1)}, u32[]{:S(2)}, u32[]{:S(2)}) collective-permute-start(bf16[2,128,256]{2,1,0:T(8,128)(2,1)S(1)} %bitcast_dynamic-update-slice_fusion.2), channel_id=1, source_target_pairs={{0,1},{1,0},{2,3},{3,2},{4,5},{5,4},{6,7},{7,6},{8,9},{9,8},{10,11... | collective-permute-start | bytes 393224 | tf_op jit(solution)/shard_map/ppermute | solution.py:18
  11.9 27.5 %collective-permute-start.6 = (bf16[2,128,256]{2,1,0:T(8,128)(2,1)S(1)}, bf16[2,128,256]{2,1,0:T(8,128)(2,1)S(1)}, u32[]{:S(2)}, u32[]{:S(2)}) collective-permute-start(bf16[2,128,256]{2,1,0:T(8,128)(2,1)S(1)} %bitcast_dynamic-update-slice_fusion), channel_id=1, source_target_pairs={{0,1},{1,0},{2,3},{3,2},{4,5},{5,4},{6,7},{7,6},{8,9},{9,8},{10,11... | collective-permute-start | bytes 393224 | tf_op jit(solution)/shard_map/ppermute | solution.py:18
  13.0 8.3 %copy-start.57 = (s32[2,2]{1,0:T(2,128)}, s32[2,2]{1,0:T(2,128)S(1)}, u32[]{:S(2)}) copy-start(s32[2,2]{1,0:T(2,128)S(1)} %iota_clamp_fusion) | copy-start | bytes 52
  13.1 8.6 %copy-start.51 = (f32[2,2]{1,0:T(2,128)}, f32[2,2]{1,0:T(2,128)S(1)}, u32[]{:S(2)}) copy-start(f32[2,2]{1,0:T(2,128)S(1)} %and_convert_fusion.8) | copy-start | bytes 52
  24.9 5.4 %copy-start.42 = (s32[2,1]{1,0:T(2,128)S(1)}, s32[2,1]{1,0:T(2,128)}, u32[]{:S(2)}) copy-start(s32[2,1]{1,0:T(2,128)} %get-tuple-element.179) | copy-start | bytes 28
  24.9 5.4 %copy-start.43 = (s32[2,1]{1,0:T(2,128)S(1)}, s32[2,1]{1,0:T(2,128)}, u32[]{:S(2)}) copy-start(s32[2,1]{1,0:T(2,128)} %get-tuple-element.180) | copy-start | bytes 28
  24.9 5.5 %copy-start.40 = (s32[2,1]{1,0:T(2,128)S(1)}, s32[2,1]{1,0:T(2,128)}, u32[]{:S(2)}) copy-start(s32[2,1]{1,0:T(2,128)} %get-tuple-element.176) | copy-start | bytes 28
  24.9 5.5 %copy-start.41 = (s32[2,1]{1,0:T(2,128)S(1)}, s32[2,1]{1,0:T(2,128)}, u32[]{:S(2)}) copy-start(s32[2,1]{1,0:T(2,128)} %get-tuple-element.177) | copy-start | bytes 28
  24.9 5.6 %copy-start.38 = (s32[2,1]{1,0:T(2,128)S(1)}, s32[2,1]{1,0:T(2,128)}, u32[]{:S(2)}) copy-start(s32[2,1]{1,0:T(2,128)} %get-tuple-element.119) | copy-start | bytes 28
  25.0 5.6 %copy-start.39 = (s32[2,1]{1,0:T(2,128)S(1)}, s32[2,1]{1,0:T(2,128)}, u32[]{:S(2)}) copy-start(s32[2,1]{1,0:T(2,128)} %get-tuple-element.120) | copy-start | bytes 28
  25.0 5.7 %copy-start.33 = (s32[2]{0:T(128)S(1)}, s32[2]{0:T(128)}, u32[]{:S(2)}) copy-start(s32[2]{0:T(128)} %copy-done.32) | copy-start | bytes 28
  25.0 5.7 %copy-start.35 = (s32[2]{0:T(128)S(1)}, s32[2]{0:T(128)}, u32[]{:S(2)}) copy-start(s32[2]{0:T(128)} %copy-done.34) | copy-start | bytes 28
  25.0 6.4 %copy-start.29 = (s32[2]{0:T(128)S(1)}, s32[2]{0:T(128)}, u32[]{:S(2)}) copy-start(s32[2]{0:T(128)} %copy-done.28) | copy-start | bytes 28
  25.0 6.4 %copy-start.31 = (s32[2]{0:T(128)S(1)}, s32[2]{0:T(128)}, u32[]{:S(2)}) copy-start(s32[2]{0:T(128)} %copy-done.30) | copy-start | bytes 28
  25.3 6.8 %copy-start.62 = (f32[2,1,128]{2,1,0:T(1,128)S(1)}, f32[2,1,128]{2,1,0:T(1,128)}, u32[]{:S(2)}) copy-start(f32[2,1,128]{2,1,0:T(1,128)} %fusion.197) | copy-start | bytes 3076
  33.1 12.7 %copy-start.61 = (f32[2,1,128]{2,1,0:T(1,128)S(1)}, f32[2,1,128]{2,1,0:T(1,128)}, u32[]{:S(2)}) copy-start(f32[2,1,128]{2,1,0:T(1,128)} %fusion.187) | copy-start | bytes 3076
  34.7 10.9 %collective-permute-start.2 = (bf16[2,256,256]{2,1,0:T(8,128)(2,1)S(1)}, bf16[2,256,256]{2,1,0:T(8,128)(2,1)S(1)}, u32[]{:S(2)}, u32[]{:S(2)}) collective-permute-start(bf16[2,256,256]{2,1,0:T(8,128)(2,1)S(1)} %maximum_select_fusion.7), channel_id=1, source_target_pairs={{0,2},{2,0},{1,3},{3,1},{4,6},{6,4},{5,7},{7,5},{8,10},{10,8},{9,1... | collective-permute-start | bytes 786440 | tf_op jit(solution)/shard_map/ppermute | solution.py:18
  38.9 58.9 %collective-permute-start.10 = (bf16[2,128,256]{2,1,0:T(8,128)(2,1)}, bf16[2,128,256]{2,1,0:T(8,128)(2,1)}, u32[]{:S(2)}, u32[]{:S(2)}) collective-permute-start(bf16[2,128,256]{2,1,0:T(8,128)(2,1)} %fusion.67), channel_id=1, source_target_pairs={{0,1},{1,0},{2,3},{3,2},{4,5},{5,4},{6,7},{7,6},{8,9},{9,8},{10,11... | collective-permute-start | bytes 393224 | tf_op jit(solution)/shard_map/ppermute | solution.py:18
  40.3 26.1 %collective-permute-start.7 = (bf16[2,256,256]{2,1,0:T(8,128)(2,1)}, bf16[2,256,256]{2,1,0:T(8,128)(2,1)}, u32[]{:S(2)}, u32[]{:S(2)}) collective-permute-start(bf16[2,256,256]{2,1,0:T(8,128)(2,1)} %maximum_select_fusion.9), channel_id=1, source_target_pairs={{0,2},{2,0},{1,3},{3,1},{4,6},{6,4},{5,7},{7,5},{8,10},{10,8},{9,1... | collective-permute-start | bytes 786440 | tf_op jit(solution)/shard_map/ppermute | solution.py:18
  43.1 14.2 %collective-permute-start.4 = (bf16[2,256,256]{2,1,0:T(8,128)(2,1)}, bf16[2,256,256]{2,1,0:T(8,128)(2,1)}, u32[]{:S(2)}, u32[]{:S(2)}) collective-permute-start(bf16[2,256,256]{2,1,0:T(8,128)(2,1)} %maximum_select_fusion.8), channel_id=1, source_target_pairs={{0,2},{2,0},{1,3},{3,1},{4,6},{6,4},{5,7},{7,5},{8,10},{10,8},{9,1... | collective-permute-start | bytes 786440 | tf_op jit(solution)/shard_map/ppermute | solution.py:18
  58.6 14.8 %collective-permute-start.5 = (bf16[2,512,256]{2,1,0:T(8,128)(2,1)S(1)}, bf16[2,512,256]{2,1,0:T(8,128)(2,1)}, u32[]{:S(2)}, u32[]{:S(2)}) collective-permute-start(bf16[2,512,256]{2,1,0:T(8,128)(2,1)S(1)} %maximum_select_fusion.4), channel_id=1, source_target_pairs={{0,4},{4,0},{1,5},{5,1},{2,6},{6,2},{3,7},{7,3},{8,12},{12,8},{9,1... | collective-permute-start | bytes 1572872 | tf_op jit(solution)/shard_map/ppermute | solution.py:18
  62.5 12.3 %copy-start.19 = (bf16[2,1,16384]{2,0,1:T(2,128)(2,1)S(1)}, bf16[2,1,16384]{2,0,1:T(2,128)(2,1)}, u32[]{:S(2)}) copy-start(bf16[2,1,16384]{2,0,1:T(2,128)(2,1)} %copy.384) | copy-start | bytes 196612
  62.5 12.3 %copy-start.27 = (f32[1,2,8,128]{3,1,2,0:T(2,128)S(1)}, f32[1,2,8,128]{3,1,2,0:T(2,128)}, u32[]{:S(2)}) copy-start(f32[1,2,8,128]{3,1,2,0:T(2,128)} %copy.393) | copy-start | bytes 24580
  62.5 12.3 %copy-start.50 = (f32[2]{0:T(128)S(1)}, f32[2]{0:T(128)}, u32[]{:S(2)}) copy-start(f32[2]{0:T(128)} %copy-done.49) | copy-start | bytes 28
  62.5 12.3 %copy-start.60 = (f32[2,1,128]{2,1,0:T(1,128)S(1)}, f32[2,1,128]{2,1,0:T(1,128)}, u32[]{:S(2)}) copy-start(f32[2,1,128]{2,1,0:T(1,128)} %fusion.177) | copy-start | bytes 3076
  63.3 36.3 %collective-permute-start.11 = (bf16[2,256,256]{2,1,0:T(8,128)(2,1)}, bf16[2,256,256]{2,1,0:T(8,128)(2,1)}, u32[]{:S(2)}, u32[]{:S(2)}) collective-permute-start(bf16[2,256,256]{2,1,0:T(8,128)(2,1)} %fusion.49), channel_id=1, source_target_pairs={{0,2},{2,0},{1,3},{3,1},{4,6},{6,4},{5,7},{7,5},{8,10},{10,8},{9,1... | collective-permute-start | bytes 786440 | tf_op jit(solution)/shard_map/ppermute | solution.py:18
  68.5 23.8 %collective-permute-start.8 = (bf16[2,512,256]{2,1,0:T(8,128)(2,1)}, bf16[2,512,256]{2,1,0:T(8,128)(2,1)}, u32[]{:S(2)}, u32[]{:S(2)}) collective-permute-start(bf16[2,512,256]{2,1,0:T(8,128)(2,1)} %maximum_select_fusion.5), channel_id=1, source_target_pairs={{0,4},{4,0},{1,5},{5,1},{2,6},{6,2},{3,7},{7,3},{8,12},{12,8},{9,1... | collective-permute-start | bytes 1572872 | tf_op jit(solution)/shard_map/ppermute | solution.py:18
  89.4 8.3 %copy-start.6 = (f32[2,256,256]{2,1,0:T(8,128)S(1)}, f32[2,256,256]{2,1,0:T(8,128)}, u32[]{:S(2)}) copy-start(f32[2,256,256]{2,1,0:T(8,128)} %copy-done.5) | copy-start | bytes 1572868
  89.6 15.5 %collective-permute-start.13 = (bf16[2,512,256]{2,1,0:T(8,128)(2,1)S(1)}, bf16[2,512,256]{2,1,0:T(8,128)(2,1)S(1)}, u32[]{:S(2)}, u32[]{:S(2)}) collective-permute-start(bf16[2,512,256]{2,1,0:T(8,128)(2,1)S(1)} %fusion.42), channel_id=1, source_target_pairs={{0,4},{4,0},{1,5},{5,1},{2,6},{6,2},{3,7},{7,3},{8,12},{12,8},{9,1... | collective-permute-start | bytes 1572872 | tf_op jit(solution)/shard_map/ppermute | solution.py:18
  94.0 29.7 %collective-permute-start.9 = (bf16[2,1024,256]{2,1,0:T(8,128)(2,1)S(1)}, bf16[2,1024,256]{2,1,0:T(8,128)(2,1)S(1)}, u32[]{:S(2)}, u32[]{:S(2)}) collective-permute-start(bf16[2,1024,256]{2,1,0:T(8,128)(2,1)S(1)} %maximum_select_fusion.2), channel_id=1, source_target_pairs={{0,8},{8,0},{1,9},{9,1},{2,10},{10,2},{3,11},{11,3},{4,12},{12,4},... | collective-permute-start | bytes 3145736 | tf_op jit(solution)/shard_map/ppermute | solution.py:18
  101.4 60.6 %collective-permute-start.12 = (bf16[2,128,256]{2,1,0:T(8,128)(2,1)}, bf16[2,128,256]{2,1,0:T(8,128)(2,1)}, u32[]{:S(2)}, u32[]{:S(2)}) collective-permute-start(bf16[2,128,256]{2,1,0:T(8,128)(2,1)} %fusion.68), channel_id=1, source_target_pairs={{0,1},{1,0},{2,3},{3,2},{4,5},{5,4},{6,7},{7,6},{8,9},{9,8},{10,11... | collective-permute-start | bytes 393224 | tf_op jit(solution)/shard_map/ppermute | solution.py:18
  105.3 19.0 %copy-start.18 = (bf16[2,1,16384]{2,0,1:T(2,128)(2,1)S(1)}, bf16[2,1,16384]{2,0,1:T(2,128)(2,1)}, u32[]{:S(2)}) copy-start(bf16[2,1,16384]{2,0,1:T(2,128)(2,1)} %copy.388) | copy-start | bytes 196612
  105.3 19.0 %copy-start.48 = (f32[2]{0:T(128)S(1)}, f32[2]{0:T(128)}, u32[]{:S(2)}) copy-start(f32[2]{0:T(128)} %copy-done.47) | copy-start | bytes 28
  105.4 19.0 %copy-start.59 = (f32[2,1,128]{2,1,0:T(1,128)S(1)}, f32[2,1,128]{2,1,0:T(1,128)}, u32[]{:S(2)}) copy-start(f32[2,1,128]{2,1,0:T(1,128)} %fusion.167) | copy-start | bytes 3076
  156.4 5.6 %copy-start.8 = (f32[2,256,256]{2,1,0:T(8,128)S(1)}, f32[2,256,256]{2,1,0:T(8,128)}, u32[]{:S(2)}) copy-start(f32[2,256,256]{2,1,0:T(8,128)} %copy-done.7) | copy-start | bytes 1572868
  158.3 24.5 %collective-permute-start.16 = (bf16[2,1024,256]{2,1,0:T(8,128)(2,1)S(1)}, bf16[2,1024,256]{2,1,0:T(8,128)(2,1)S(1)}, u32[]{:S(2)}, u32[]{:S(2)}) collective-permute-start(bf16[2,1024,256]{2,1,0:T(8,128)(2,1)S(1)} %fusion.36), channel_id=1, source_target_pairs={{0,8},{8,0},{1,9},{9,1},{2,10},{10,2},{3,11},{11,3},{4,12},{12,4},... | collective-permute-start | bytes 3145736 | tf_op jit(solution)/shard_map/ppermute | solution.py:18
  158.5 8.8 %collective-permute-start.14 = (bf16[2,256,256]{2,1,0:T(8,128)(2,1)S(1)}, bf16[2,256,256]{2,1,0:T(8,128)(2,1)S(1)}, u32[]{:S(2)}, u32[]{:S(2)}) collective-permute-start(bf16[2,256,256]{2,1,0:T(8,128)(2,1)S(1)} %fusion.50), channel_id=1, source_target_pairs={{0,2},{2,0},{1,3},{3,1},{4,6},{6,4},{5,7},{7,5},{8,10},{10,8},{9,1... | collective-permute-start | bytes 786440 | tf_op jit(solution)/shard_map/ppermute | solution.py:18
  161.8 21.0 %copy-start = (f32[2,1,1024,256]{3,2,0,1:T(8,128)S(1)}, f32[2,1,1024,256]{3,2,0,1:T(8,128)}, u32[]{:S(2)}) copy-start(f32[2,1,1024,256]{3,2,0,1:T(8,128)} %copy.158) | copy-start | bytes 6291460
  167.4 16.4 %copy-start.12 = (bf16[2,1024,256]{2,1,0:T(8,128)(2,1)S(1)}, bf16[2,1024,256]{2,1,0:T(8,128)(2,1)}, u32[]{:S(2)}) copy-start(bf16[2,1024,256]{2,1,0:T(8,128)(2,1)} %copy-done.11) | copy-start | bytes 3145732
  167.4 16.4 %copy-start.16 = (bf16[2,128,1024]{2,1,0:T(8,128)(2,1)S(1)}, bf16[2,128,1024]{2,1,0:T(8,128)(2,1)}, u32[]{:S(2)}) copy-start(bf16[2,128,1024]{2,1,0:T(8,128)(2,1)} %copy-done.15) | copy-start | bytes 1572868
  167.4 16.8 %collective-permute-start.15 = (bf16[2,128,256]{2,1,0:T(8,128)(2,1)S(1)}, bf16[2,128,256]{2,1,0:T(8,128)(2,1)S(1)}, u32[]{:S(2)}, u32[]{:S(2)}) collective-permute-start(bf16[2,128,256]{2,1,0:T(8,128)(2,1)S(1)} %fusion.69), channel_id=1, source_target_pairs={{0,1},{1,0},{2,3},{3,2},{4,5},{5,4},{6,7},{7,6},{8,9},{9,8},{10,11... | collective-permute-start | bytes 393224 | tf_op jit(solution)/shard_map/ppermute | solution.py:18
  183.3 9.3 %collective-permute-start.17 = (bf16[2,512,256]{2,1,0:T(8,128)(2,1)S(1)}, bf16[2,512,256]{2,1,0:T(8,128)(2,1)S(1)}, u32[]{:S(2)}, u32[]{:S(2)}) collective-permute-start(bf16[2,512,256]{2,1,0:T(8,128)(2,1)S(1)} %fusion.43), channel_id=1, source_target_pairs={{0,4},{4,0},{1,5},{5,1},{2,6},{6,2},{3,7},{7,3},{8,12},{12,8},{9,1... | collective-permute-start | bytes 1572872 | tf_op jit(solution)/shard_map/ppermute | solution.py:18
  185.6 11.7 %copy-start.20 = (f32[2,2,16384]{2,1,0:T(2,128)S(1)}, f32[2,2,16384]{2,1,0:T(2,128)}, u32[]{:S(2)}) copy-start(f32[2,2,16384]{2,1,0:T(2,128)} %reshape_reshape_transpose.2) | copy-start | bytes 786436
  185.6 11.7 %copy-start.26 = (f32[1,2,128,128]{3,1,2,0:T(2,128)S(1)}, f32[1,2,128,128]{3,1,2,0:T(2,128)}, u32[]{:S(2)}) copy-start(f32[1,2,128,128]{3,1,2,0:T(2,128)} %copy.373) | copy-start | bytes 393220
  185.6 11.7 %copy-start.52 = (f32[2,2]{1,0:T(2,128)S(1)}, f32[2,2]{1,0:T(2,128)}, u32[]{:S(2)}) copy-start(f32[2,2]{1,0:T(2,128)} %copy-done.51) | copy-start | bytes 52
  185.6 11.7 %copy-start.53 = (f32[2,2]{1,0:T(2,128)S(1)}, f32[2,2]{1,0:T(2,128)}, u32[]{:S(2)}) copy-start(f32[2,2]{1,0:T(2,128)} %get-tuple-element.207) | copy-start | bytes 52
  185.6 11.7 %copy-start.54 = (f32[2,2]{1,0:T(2,128)S(1)}, f32[2,2]{1,0:T(2,128)}, u32[]{:S(2)}) copy-start(f32[2,2]{1,0:T(2,128)} %get-tuple-element.208) | copy-start | bytes 52
  185.6 11.7 %copy-start.55 = (f32[2,2]{1,0:T(2,128)S(1)}, f32[2,2]{1,0:T(2,128)}, u32[]{:S(2)}) copy-start(f32[2,2]{1,0:T(2,128)} %get-tuple-element.203) | copy-start | bytes 52
  185.6 11.7 %copy-start.56 = (f32[2,2]{1,0:T(2,128)S(1)}, f32[2,2]{1,0:T(2,128)}, u32[]{:S(2)}) copy-start(f32[2,2]{1,0:T(2,128)} %get-tuple-element.204) | copy-start | bytes 52
  185.6 11.7 %copy-start.58 = (s32[2,2]{1,0:T(2,128)S(1)}, s32[2,2]{1,0:T(2,128)}, u32[]{:S(2)}) copy-start(s32[2,2]{1,0:T(2,128)} %copy-done.57) | copy-start | bytes 52
  193.5 55.1 %collective-permute-start.18 = (bf16[2,256,256]{2,1,0:T(8,128)(2,1)}, bf16[2,256,256]{2,1,0:T(8,128)(2,1)S(1)}, u32[]{:S(2)}, u32[]{:S(2)}) collective-permute-start(bf16[2,256,256]{2,1,0:T(8,128)(2,1)} %fusion.51), channel_id=1, source_target_pairs={{0,2},{2,0},{1,3},{3,1},{4,6},{6,4},{5,7},{7,5},{8,10},{10,8},{9,1... | collective-permute-start | bytes 786440 | tf_op jit(solution)/shard_map/ppermute | solution.py:18
  198.6 51.5 %copy-start.37 = (f32[256]{0:T(256)S(1)}, f32[256]{0:T(256)}, u32[]{:S(2)}) copy-start(f32[256]{0:T(256)} %param.13) | copy-start | bytes 3076
  199.3 54.7 %copy-start.17 = (f32[2,2,32768]{2,1,0:T(2,128)S(1)}, f32[2,2,32768]{2,1,0:T(2,128)}, u32[]{:S(2)}) copy-start(f32[2,2,32768]{2,1,0:T(2,128)} %reshape.1667) | copy-start | bytes 1572868
  199.3 54.7 %copy-start.21 = (f32[1,2,128,256]{3,1,2,0:T(2,128)S(1)}, f32[1,2,128,256]{3,1,2,0:T(2,128)}, u32[]{:S(2)}) copy-start(f32[1,2,128,256]{3,1,2,0:T(2,128)} %copy.191) | copy-start | bytes 786436
  199.3 54.7 %copy-start.22 = (f32[1,2,128,256]{3,1,2,0:T(2,128)S(1)}, f32[1,2,128,256]{3,1,2,0:T(2,128)}, u32[]{:S(2)}) copy-start(f32[1,2,128,256]{3,1,2,0:T(2,128)} %copy.192) | copy-start | bytes 786436
  248.8 5.0 %collective-permute-start.19 = (bf16[2,128,256]{2,1,0:T(8,128)(2,1)S(1)}, bf16[2,128,256]{2,1,0:T(8,128)(2,1)S(1)}, u32[]{:S(2)}, u32[]{:S(2)}) collective-permute-start(bf16[2,128,256]{2,1,0:T(8,128)(2,1)S(1)} %fusion.70), channel_id=1, source_target_pairs={{0,1},{1,0},{2,3},{3,2},{4,5},{5,4},{6,7},{7,6},{8,9},{9,8},{10,11... | collective-permute-start | bytes 393224 | tf_op jit(solution)/shard_map/ppermute | solution.py:18
  (19 other events, 52.2 us)
